TPU v7x, 128 devices: a whole 4x4x4 slice. The times are simulated.
128 devices in a mesh: row: 16 (over x, y_lo, core), col: 8 (over y_hi, z).
Axes of the slice: x: 4, y: 4 (y_hi: 2, y_lo: 2; y = y_hi * 2 + y_lo), z: 4, core: 2. Of those that a mesh axis runs over, the one named last changes fastest.
Arguments:
- hidden_states: bfloat16 [16384, 2048], P('row', 'col'), may hold values from -21 to 21
- lengths: int32 [32], P('row'), may hold values from 16 to 512, as said below
- qkvg_master: float32 [2048, 12288], P(('row', 'col')), may hold values from -0.125 to 0.125
- gateup_master: float32 [2, 2048, 4096], P(None, ('row', 'col')), may hold values from -0.125 to 0.125
- out_master: float32 [4096, 2048], P(None, ('row', 'col')), may hold values from -0.09375 to 0.09375
- down_master: float32 [4096, 2048], P(None, ('row', 'col')), may hold values from -0.09375 to 0.09375
Outputs:
- layer_output: bfloat16 [16384, 2048], P('row', 'col')
- qkvg_weight: bfloat16 [2048, 12288], P('row', 'col')
- gateup_weight: bfloat16 [2, 2048, 4096], P(None, 'row', 'col')
- mixing_weight: bfloat16 [4096, 2048], P('col', 'row')
- down_weight: bfloat16 [4096, 2048], P('col', 'row')
Inputs may be any that keep to these rules, and one draw needn't show every extreme that they name: `lengths`: prompt length of each request; the positions of a request from its length on are padding. Some request has length 512 in every draw.
All inputs are finite; a program needn't handle non-finite values.
Results may differ from a plain program's by a relative error of at most 0.014.
Values may be sent and summed in bfloat16 or wider, within the bound.
A program may use at most 128 MiB of HBM per device.

v0:
```python
import math
import jax
import jax.numpy as jnp
from jax import lax
from jax.sharding import PartitionSpec as P

D = 2048
HEADS = 8
KEY = 256
VAL = 512
S = 512
BLOCK = 256
epsilon = 1e-05


def rms_round(values):
    scale = lax.rsqrt(jnp.mean(values * values, axis=-1, keepdims=True) + epsilon)
    return (values * scale).astype(jnp.bfloat16)


def rotate(values, positions):
    half = values.shape[-1] // 2
    freq = jnp.power(10000.0, -2.0 * jnp.arange(half).astype(jnp.float32) / values.shape[-1])
    angle = positions.astype(jnp.float32)[:, None] * freq[None, :]
    cosine = jnp.cos(angle)[:, None, :]
    sine = jnp.sin(angle)[:, None, :]
    first = values[..., :half]
    second = values[..., half:]
    return jnp.concatenate(
        [first * cosine - second * sine, first * sine + second * cosine], axis=-1
    )


def retain(gammas, query, keyed, value):
    heads = query.shape[1]
    blocks = S // BLOCK
    offsets = jnp.arange(BLOCK)
    lag = offsets[:, None] - offsets[None, :]
    within = jnp.where(
        (lag >= 0)[None],
        jnp.power(gammas[:, None, None], jnp.maximum(lag, 0).astype(jnp.float32)[None]),
        0.0,
    )
    into = jnp.power(gammas[:, None], (offsets + 1).astype(jnp.float32)[None, :])
    leaving = jnp.power(gammas[:, None], (BLOCK - 1 - offsets).astype(jnp.float32)[None, :])
    across_blocks_sum = jnp.power(gammas, 1.0 * BLOCK)
    upper_bound = lax.Precision.HIGHEST

    def advance(carry, inputs):
        retention_state, key_sum = carry
        query_block, key_block, value_tile_rows = inputs
        scores = (
            jnp.einsum("thk,shk->hts", query_block, key_block, preferred_element_type=jnp.float32)
            * within
        )
        denom_inside = jnp.sum(scores, axis=2)
        inside = jnp.einsum(
            "hts,shv->thv",
            scores.astype(jnp.bfloat16),
            value_tile_rows,
            preferred_element_type=jnp.float32,
        )
        damped_query_rows = query_block.astype(jnp.float32) * jnp.transpose(into)[:, :, None]
        carried_state = jnp.einsum(
            "swc,wcm->swm", damped_query_rows, retention_state, precision=upper_bound
        )
        denom_carried = jnp.einsum("thk,hk->th", damped_query_rows, key_sum, precision=upper_bound)
        damped_key_rows = key_block.astype(jnp.float32) * jnp.transpose(leaving)[:, :, None]
        retention_state = across_blocks_sum[:, None, None] * retention_state + jnp.einsum(
            "wat,wag->atg",
            damped_key_rows,
            value_tile_rows.astype(jnp.float32),
            precision=upper_bound,
        )
        key_sum = across_blocks_sum[:, None] * key_sum + jnp.sum(damped_key_rows, axis=0)
        denom = jnp.transpose(denom_inside) + denom_carried
        result = (inside + carried_state) / jnp.maximum(jnp.abs(denom), 1.0)[:, :, None]
        return ((retention_state, key_sum), result)

    start = (jnp.zeros((heads, KEY, VAL), jnp.float32), jnp.zeros((heads, KEY), jnp.float32))
    sliced = (
        query.reshape(blocks, BLOCK, heads, KEY),
        keyed.reshape(blocks, BLOCK, heads, KEY),
        value.reshape(blocks, BLOCK, heads, VAL),
    )
    _, results = lax.scan(advance, start, sliced)
    return results.reshape(S, heads, VAL)


def gate_heads(retained, gate):
    centre = jnp.mean(retained, axis=-1, keepdims=True)
    centred = retained - centre
    spread = jnp.mean(centred * centred, axis=-1, keepdims=True)
    grouped = centred * lax.rsqrt(spread + epsilon)
    return (jax.nn.silu(gate.astype(jnp.float32)) * grouped).astype(jnp.bfloat16)


def shards(hidden_states, lengths, qkvg_master, gateup_master, out_master, down_master):
    tok_rows = hidden_states.shape[0]
    share_width = hidden_states.shape[1]
    requests = lengths.shape[0]
    head_count = HEADS // lax.axis_size("col")
    head_width = 2 * KEY + 2 * VAL
    in_blocks = (
        lax.all_to_all(
            qkvg_master.astype(jnp.bfloat16)[None], "col", split_axis=2, concat_axis=1, tiled=True
        ),
        lax.all_to_all(
            gateup_master.astype(jnp.bfloat16), "col", split_axis=2, concat_axis=1, tiled=True
        ),
    )
    qkvg_blocks = in_blocks[0][0]
    gateup_blocks = in_blocks[1]
    out_blocks, down_blocks = (
        lax.all_to_all(
            out_master.astype(jnp.bfloat16), "col", split_axis=0, concat_axis=1, tiled=True
        ),
        lax.all_to_all(
            down_master.astype(jnp.bfloat16), "col", split_axis=0, concat_axis=1, tiled=True
        ),
    )
    gathered = lax.all_gather(hidden_states, "col", axis=1, tiled=True)
    normed = rms_round(gathered.astype(jnp.float32))
    columns = normed
    projected = jnp.dot(
        columns,
        lax.all_gather(qkvg_blocks, "row", axis=0, tiled=True),
        preferred_element_type=jnp.float32,
    )
    projected = projected.astype(jnp.bfloat16).reshape(requests, S, head_count, head_width)
    positions = jnp.arange(S)
    query = rotate(projected[..., :KEY].astype(jnp.float32), positions).astype(jnp.bfloat16)
    keyed = (
        rotate(projected[..., KEY : 2 * KEY].astype(jnp.float32), positions)
        * (1.0 / math.sqrt(KEY))
    ).astype(jnp.bfloat16)
    value = projected[..., 2 * KEY : 2 * KEY + VAL]
    gate = projected[..., 2 * KEY + VAL :]
    head_ids = lax.axis_index("col") * head_count + jnp.arange(head_count)
    gammas = 1.0 - jnp.power(2.0, -5.0 - head_ids.astype(jnp.float32))
    retained = jax.vmap(retain, in_axes=(None, 0, 0, 0))(gammas, query, keyed, value)
    mixed = gate_heads(retained, gate).reshape(tok_rows, head_count * VAL)
    partial_mix = jnp.dot(
        mixed,
        lax.all_gather(out_blocks, "row", axis=1, tiled=True),
        preferred_element_type=jnp.float32,
    )
    residual = hidden_states.astype(jnp.float32) + lax.psum_scatter(
        partial_mix.astype(jnp.bfloat16), "col", scatter_dimension=1, tiled=True
    ).astype(jnp.float32)
    squares = lax.psum(jnp.sum(residual * residual, axis=1), "col")
    normed_share = (residual * lax.rsqrt(squares[:, None] / D + epsilon)).astype(jnp.bfloat16)
    normed_mid = lax.all_gather(normed_share, "col", axis=1, tiled=True)
    columns = normed_mid
    paired = jnp.einsum(
        "td,gdf->gtf",
        columns,
        lax.all_gather(gateup_blocks, "row", axis=1, tiled=True),
        preferred_element_type=jnp.float32,
    )
    hidden = (jax.nn.silu(paired[0]) * paired[1]).astype(jnp.bfloat16)
    partial_feed = jnp.dot(
        hidden,
        lax.all_gather(down_blocks, "row", axis=1, tiled=True),
        preferred_element_type=jnp.float32,
    )
    feed = lax.psum_scatter(
        partial_feed.astype(jnp.bfloat16), "col", scatter_dimension=1, tiled=True
    ).astype(jnp.float32)
    live = positions[None, :] < lengths[:, None]
    summed = (residual + feed).reshape(requests, S, share_width)
    layer_output = (
        jnp.where(live[:, :, None], summed, 0.0).astype(jnp.bfloat16).reshape(tok_rows, share_width)
    )
    return (layer_output, qkvg_blocks, gateup_blocks, out_blocks, down_blocks)


def solution(mesh):
    return jax.shard_map(
        shards,
        mesh=mesh,
        in_specs=(
            P("row", "col"),
            P("row"),
            P(("row", "col"), None),
            P(None, ("row", "col"), None),
            P(None, ("row", "col")),
            P(None, ("row", "col")),
        ),
        out_specs=(
            P("row", "col"),
            P("row", "col"),
            P(None, "row", "col"),
            P("col", "row"),
            P("col", "row"),
        ),
        check_vma=False,
    )
```

profile of v0, /device:TPU:0, one launch (start us, length us, event | category | flops | bytes accessed | tf_op | source)
XLA Modules:
  0.0 546.4 jit_solution(4470054809173031747)
XLA Ops:
  7.2 0.7 all-gather.7.cloned.1.call-update
  7.9 1.2 convert_bitcast_fusion
  9.1 9.8 %copy.81 = bf16[1,16,12288]{1,0,2:T(2,128)(2,1)} copy(bf16[1,16,12288]{2,1,0:T(8,128)(2,1)S(1)} %convert_bitcast_fusion) | data formatting | bytes 786432 | tf_op jit(solution)/shard_map/broadcast_in_dim | solution.py:106
  18.9 0.5 broadcast.312
  19.4 67.0 %reduce.7 = bf16[12288,16]{1,0:T(8,128)(2,1)S(1)} reduce(bf16[12288,1,16]{2,1,0:T(2,128)(2,1)} %bitcast.202, bf16[]{:T(256)} %broadcast.312), dimensions={1}, to_apply=%bitcast.147.reduce_sub_computation | reduce | bytes 786434
  86.4 3.3 reshape.460
  89.7 18.0 %all_to_all.71 = bf16[8,2,12288]{2,1,0:T(2,128)(2,1)S(1)} all-to-all(bf16[8,2,12288]{2,1,0:T(2,128)(2,1)S(1)} %reshape.460), channel_id=1, replica_groups=mesh['row'=16,'col'=8] {'col'}, dimensions={0} | all-to-all | bytes 786432 | tf_op jit(solution)/shard_map/all_to_all | solution.py:105
  107.7 6.2 %reshape.461 = bf16[12288,1,16]{2,1,0:T(2,128)(2,1)} reshape(bf16[8,2,12288]{2,1,0:T(2,128)(2,1)S(1)} %all_to_all.71) | data formatting | bytes 786432
  114.0 11.4 %copy.82 = bf16[1,16,12288]{2,1,0:T(8,128)(2,1)S(1)} copy(bf16[1,16,12288]{1,0,2:T(2,128)(2,1)} %bitcast.203) | data formatting | bytes 786432 | tf_op jit(solution)/shard_map/all_to_all | solution.py:105
  125.6 0.9 copy.83
  126.5 0.7 copy.118
  127.1 3.4 all-to-all-start.1
  130.6 1.0 multiply_cosine_fusion
  131.7 6.8 %all-to-all-done.1 = bf16[8,512,16]{1,2,0:T(8,128)(2,1)S(1)} async-done(((bf16[8,512,16]{1,2,0:T(8,128)(2,1)}), bf16[8,512,16]{1,2,0:T(8,128)(2,1)S(1)}, u32[]{:S(2)}, u32[]{:S(2)}) %all-to-all-start.1) | async-done | bytes 131104 | tf_op jit(solution)/shard_map/all_to_all | solution.py:115
  138.5 0.7 copy-done.6
  139.5 3.1 fusion.45
  142.6 23.4 %all-gather.9.cloned.1.call-done = bf16[2048,1536]{1,0:T(8,128)(2,1)} async-done(((bf16[128,1536]{1,0:T(8,128)(2,1)}), bf16[2048,1536]{1,0:T(8,128)(2,1)}) %all-gather.9.cloned.1.call-update) | async-done | bytes 6291472 | tf_op jit(solution)/shard_map/all_gather | solution.py:127
  166.1 10.5 %fusion.52 = bf16[1024,1536]{1,0:T(8,128)(2,1)S(1)} fusion(bf16[2048,1536]{1,0:T(8,128)(2,1)} %all-gather.9.cloned.1.call-done, bf16[1024,2048]{1,0:T(8,128)(2,1)} %all-gather.7.cloned.1.call-done, f32[1024]{0:T(1024)S(1)} %add_rsqrt_fusion.1), kind=kOutput, calls=%fused_computation.65 | convolution fusion | flops 6450315264 | bytes 13635584 | tf_op jit(solution)/shard_map/dot_general | solution.py:125
  176.8 1.4 copy-done.5
  178.2 0.3 subtract_convert_fusion
  178.6 18.9 %while.17 = (s32[]{:T(128)}, f32[2,1,256,512]{3,2,0,1:T(8,128)S(1)}, f32[2,1,256]{2,1,0:T(1,128)S(1)}, f32[2,2,256,1,512]{4,2,0,1,3:T(8,128)}, f32[1]{0:T(128)},...) while((s32[]{:T(128)}, ...), condition=%wide.region_4.5_spmd.clone.clone.clone, body=%wide.region_1.4_spmd.clone.clone.clone.sunk | while | flops 1816989184 | bytes 22576332 | solution.py:86
  178.7 0.6 fusion.101
  179.3 0.3 select_bitcast_fusion.2
  179.7 0.3 fusion.100
  180.0 2.0 convolution_bitcast_fusion.3
  181.9 1.3 divide_bitcast_fusion.2
  183.3 1.6 copy.122
  184.8 1.1 constant_dynamic-update-slice_fusion.2
  185.9 2.0 fusion.98
  188.1 0.6 fusion.101
  188.8 0.3 select_bitcast_fusion.2
  189.1 0.3 fusion.100
  189.4 2.0 convolution_bitcast_fusion.3
  191.4 1.3 divide_bitcast_fusion.2
  192.7 1.6 copy.122
  194.3 1.1 constant_dynamic-update-slice_fusion.2
  195.4 2.0 fusion.98
  197.5 2.0 bitcast_reduce_fusion
  199.5 0.3 copy-done
  199.8 0.4 fusion.66
  200.3 2.1 fusion.67
  202.4 0.8 all-gather.11.cloned.1.call-done
  203.2 5.9 %convolution_convert_fusion.1 = bf16[1024,2048]{1,0:T(8,128)(2,1)} fusion(bf16[1024,512]{1,0:T(8,128)(2,1)S(1)} %bitcast.224, bf16[512,2048]{0,1:T(8,128)(2,1)} %all-gather.11.cloned.1.call-done), kind=kOutput, calls=%fused_computation.67 | convolution fusion | flops 2149580800 | bytes 7340032 | tf_op jit(solution)/shard_map/dot_general | solution.py:143
  209.5 0.7 copy-done.9
  210.2 2.7 copy.89
  213.0 2.2 reshape.458
  215.2 17.3 %all_to_all.72 = bf16[8,2,8192]{2,1,0:T(2,128)(2,1)S(1)} all-to-all(bf16[8,2,8192]{2,1,0:T(2,128)(2,1)S(1)} %reshape.458), channel_id=1, replica_groups=mesh['row'=16,'col'=8] {'col'}, dimensions={0} | all-to-all | bytes 524288 | tf_op jit(solution)/shard_map/all_to_all | solution.py:108
  232.5 1.4 reshape.459
  233.9 3.3 copy.90
  237.2 59.2 %reduce-scatter.3.cloned.1.call-done = bf16[1024,256]{1,0:T(8,128)(2,1)} async-done(((bf16[1024,2048]{1,0:T(8,128)(2,1)}), bf16[1024,256]{1,0:T(8,128)(2,1)}) %reduce-scatter.3.cloned.1.call-update) | async-done | bytes 524304 | tf_op jit(solution)/shard_map/reduce_scatter | solution.py:148
  296.5 1.3 multiply_reduce_fusion
  297.8 21.4 %psum.7 = f32[1024]{0:T(1024)S(1)} all-reduce(f32[1024]{0:T(1024)S(1)} %multiply_reduce_fusion), channel_id=1, replica_groups=mesh['row'=16,'col'=8] {'col'}, use_global_device_ids=true, to_apply=%region_9.10 | all-reduce | flops 1024 | bytes 8192 | tf_op jit(solution)/shard_map/psum | solution.py:151
  319.2 2.1 multiply_convert_fusion
  321.4 12.9 %all_to_all.73 = bf16[8,512,16]{1,2,0:T(8,128)(2,1)} all-to-all(bf16[8,512,16]{1,2,0:T(8,128)(2,1)S(1)} %bitcast.227), channel_id=1, replica_groups=mesh['row'=16,'col'=8] {'col'}, dimensions={0} | all-to-all | bytes 262144 | tf_op jit(solution)/shard_map/all_to_all | solution.py:118
  334.3 1.0 all-gather.15.cloned.1.call-done
  335.3 76.4 %all-gather.13.cloned.1.call-done = bf16[1024,2048]{1,0:T(8,128)(2,1)} async-done(((bf16[1024,256]{1,0:T(8,128)(2,1)}), bf16[1024,2048]{1,0:T(8,128)(2,1)}) %all-gather.13.cloned.1.call-update) | async-done | bytes 4194320 | tf_op jit(solution)/shard_map/all_gather | solution.py:153
  411.7 9.9 %fusion.55 = f32[2,1024,512]{2,1,0:T(8,128)} fusion(bf16[2,2048,512]{2,1,0:T(8,128)(2,1)} %all-gather.15.cloned.1.call-done, bf16[1024,2048]{1,0:T(8,128)(2,1)} %all-gather.13.cloned.1.call-done), kind=kOutput, calls=%fused_computation.70 | convolution fusion | flops 4294967296 | bytes 12582912 | tf_op jit(solution)/shard_map/td,gdf->gtf/dot_general | solution.py:155
  421.6 23.7 %all-gather.17.cloned.1.call-done = bf16[512,2048]{0,1:T(8,128)(2,1)} async-done(((bf16[512,128]{0,1:T(8,128)(2,1)}), bf16[512,2048]{0,1:T(8,128)(2,1)}) %all-gather.17.cloned.1.call-update) | async-done | bytes 2097168 | tf_op jit(solution)/shard_map/all_gather | solution.py:164
  445.3 7.2 %convolution_convert_fusion = bf16[1024,2048]{1,0:T(8,128)(2,1)} fusion(bf16[512,2048]{0,1:T(8,128)(2,1)} %all-gather.17.cloned.1.call-done, f32[2,1024,512]{2,1,0:T(8,128)} %fusion.55), kind=kOutput, calls=%fused_computation.66 | convolution fusion | flops 2152726528 | bytes 10485760 | tf_op jit(solution)/shard_map/dot_general | solution.py:162
  452.5 0.6 copy-done.12
  453.4 0.8 copy.92
  454.1 0.8 copy.93
  454.9 82.5 %reduce-scatter.5.cloned.1.call-done = bf16[1024,256]{1,0:T(8,128)(2,1)} async-done(((bf16[1024,2048]{1,0:T(8,128)(2,1)}), bf16[1024,256]{1,0:T(8,128)(2,1)}) %reduce-scatter.5.cloned.1.call-update) | async-done | bytes 524304 | tf_op jit(solution)/shard_map/reduce_scatter | solution.py:167
  537.4 2.1 select_convert_fusion
  (72 shorter events, 2.2 us)
Async XLA Ops:
  7.2 132.3 %all-gather.7.cloned.1.call-start = ((), (), s32[]{:S(2)}) async-start(), calls=%async_computation.6 | async-start | bytes 4718592 | tf_op jit(solution)/shard_map/all_gather | solution.py:122
  7.9 158.2 %all-gather.9.cloned.1.call-start = ((), (), s32[]{:S(2)}) async-start(), calls=%async_computation.7 | async-start | bytes 6684672 | tf_op jit(solution)/shard_map/all_gather | solution.py:127
  125.4 1.1 copy-start.10
  127.1 11.4 %all-to-all-start.1 = ((bf16[8,512,16]{1,2,0:T(8,128)(2,1)}), bf16[8,512,16]{1,2,0:T(8,128)(2,1)S(1)}, u32[]{:S(2)}, u32[]{:S(2)}) async-start(bf16[8,512,16]{1,2,0:T(8,128)(2,1)} %bitcast.160), calls=%async_computation.1 | async-start | bytes 262144 | tf_op jit(solution)/shard_map/all_to_all | solution.py:115
  130.5 72.7 %all-gather.11.cloned.1.call-start = ((), (), s32[]{:S(2)}) async-start(), calls=%async_computation.8 | async-start | bytes 2228224 | tf_op jit(solution)/shard_map/all_gather | solution.py:145
  138.5 0.7 copy-start.6
  139.2 157.3 %reduce-scatter.3.cloned.1.call-start = ((), (), s32[]{:S(2)}) async-start(), calls=%async_computation.9 | async-start | bytes 4718592 | tf_op jit(solution)/shard_map/reduce_scatter | solution.py:148
  176.6 1.7 copy-start.5
  178.6 3.3 copy-start.1
  185.9 2.1 copy-start.2
  188.1 3.3 copy-start.1
  195.4 2.2 copy-start.2
  197.5 2.3 copy-start
  209.2 1.0 copy-start.9
  209.2 126.1 %all-gather.15.cloned.1.call-start = ((), (), s32[]{:S(2)}) async-start(), calls=%async_computation.11 | async-start | bytes 4456448 | tf_op jit(solution)/shard_map/all_gather | solution.py:158
  232.5 64.0 %copy-start.3 = (bf16[1024,256]{1,0:T(8,128)(2,1)S(1)}, bf16[1024,256]{1,0:T(8,128)(2,1)}, u32[]{:S(2)}) copy-start(bf16[1024,256]{1,0:T(8,128)(2,1)} %param.8) | copy-start | bytes 1572868
  237.2 84.1 %copy-start.11 = (f32[4096,16]{0,1:T(8,128)S(1)}, f32[4096,16]{0,1:T(8,128)}, u32[]{:S(2)}) copy-start(f32[4096,16]{0,1:T(8,128)} %param.13) | copy-start | bytes 786436
  237.2 174.5 %all-gather.13.cloned.1.call-start = ((), (), s32[]{:S(2)}) async-start(), calls=%async_computation.10 | async-start | bytes 4718592 | tf_op jit(solution)/shard_map/all_gather | solution.py:153
  321.3 124.0 %all-gather.17.cloned.1.call-start = ((), (), s32[]{:S(2)}) async-start(), calls=%async_computation.12 | async-start | bytes 2228224 | tf_op jit(solution)/shard_map/all_gather | solution.py:164
  334.3 203.2 %reduce-scatter.5.cloned.1.call-start = ((), (), s32[]{:S(2)}) async-start(), calls=%async_computation.13 | async-start | bytes 4718592 | tf_op jit(solution)/shard_map/reduce_scatter | solution.py:167
  452.5 0.7 copy-start.12
  452.5 0.9 copy-start.7
  452.5 1.7 copy-start.8
  452.5 85.0 %copy-start.4 = (bf16[1024,256]{1,0:T(8,128)(2,1)S(1)}, bf16[1024,256]{1,0:T(8,128)(2,1)}, u32[]{:S(2)}) copy-start(bf16[1024,256]{1,0:T(8,128)(2,1)} %reduce-scatter.3.cloned.1.call-done) | copy-start | bytes 1572868
Sparse Core Ops, SparseCore 0:
  10.2 76.3 all-gather.6
  126.6 39.4 all-gather.8
  168.3 34.8 all-gather.10
  209.3 87.1 reduce-scatter.2
  298.7 36.6 all-gather.14
  338.2 73.4 all-gather.12
  413.5 31.7 all-gather.16
  452.6 84.7 reduce-scatter.4
where the time goes:
time: 547 us; the launch traced here: 546 us
  waiting for transfers between devices  275 us (50%)
  other arithmetic  84 us (15%)
  blocking collectives  69.6 us (13%)
  local copies, waits for them, and re-layouts  53.3 us (10%)
  matrix products  46 us (8%)
  between operations  14.5 us (3%)
    reduce_scatter x1, waiting for transfers between devices, shards(): lax.psum_scatter(partial_feed.astype(jnp.bfloat16), 'col', scatter_dimens...  82.5 us
    all_gather x1, waiting for transfers between devices, shards(): normed_mid = lax.all_gather(normed_share, 'col', axis=1, tiled=True)  76.4 us
    unnamed x5, other arithmetic  67 us
    reduce_scatter x1, waiting for transfers between devices, shards(): lax.psum_scatter(partial_mix.astype(jnp.bfloat16), 'col', scatter_dimensi...  59.2 us
    all_gather x1, waiting for transfers between devices, shards(): lax.all_gather(down_blocks, 'row', axis=1, tiled=True)  23.7 us
    all_gather x1, waiting for transfers between devices, shards(): lax.all_gather(qkvg_blocks, 'row', axis=0, tiled=True)  23.4 us
    psum x1, blocking collectives, shards(): squares = lax.psum(jnp.sum(residual * residual, axis=1), 'col')  21.4 us
    unnamed x32, local copies, waits for them, and re-layouts  19.1 us
  transfers between devices with their start and end apart: 9, of which 8 were waited for; matrix products, arithmetic and copies ran while one was open for 30% of the time, Pallas kernels for 0%

commit v1 on v0

--- a/solution.py
+++ b/solution.py
@@ -124,7 +124,9 @@
     columns = normed
     projected = jnp.dot(
         columns,
-        lax.all_gather(qkvg_blocks, "row", axis=0, tiled=True),
+        jnp.concatenate(
+            lax.all_to_all(jnp.stack([qkvg_blocks] * lax.axis_size("row")), "row", 0, 0), axis=0
+        ),
         preferred_element_type=jnp.float32,
     )
     projected = projected.astype(jnp.bfloat16).reshape(requests, S, head_count, head_width)

time: 547 us -> 623 us (1.14)
  waiting for transfers between devices: 275 us -> 351 us
  blocking collectives: 69.6 us -> 53.6 us
  starting transfers between devices: 4.1 us -> 16.8 us
    all_to_all x0 -> x2, waiting for transfers between devices: none -> 107 us  [the longest x1 97.8 us: shards(): lax.all_to_all(jnp.stack([qkvg_blocks] * lax.axis_size('row')), 'row', 0, 0)]
    all_gather x1 -> x0, waiting for transfers between devices: 23.4 us -> none  [shards(): lax.all_gather(qkvg_blocks, 'row', axis=0, tiled=True)]
    all_to_all x1 -> x0, blocking collectives: 18 us -> none  [shards(): lax.all_to_all(qkvg_master.astype(jnp.bfloat16)[None], 'col', split_axis=...]
    all_to_all x0 -> x2, starting transfers between devices: none -> 12.7 us  [the longest x1 8.06 us: shards(): lax.all_to_all(qkvg_master.astype(jnp.bfloat16)[None], 'col', split_axis=...]
    all_to_all x1, waiting for transfers between devices: 6.84 us -> 0.01 us  [shards(): lax.all_to_all(out_master.astype(jnp.bfloat16), 'col', split_axis=0, conc...]
    unnamed x32 -> x34, local copies, waits for them, and re-layouts: 19.1 us -> 19.1 us
  transfers between devices with their start and end apart: 9 -> 10, of which waited for: 8 -> 7; matrix products, arithmetic and copies ran while one was open for 30% -> 27% of each run, Pallas kernels for 0% -> 0%
where the time goes in v1:
time: 623 us; the launch traced here: 622 us
  waiting for transfers between devices  351 us (56%)
  other arithmetic  83.9 us (13%)
  local copies, waits for them, and re-layouts  55.7 us (9%)
  blocking collectives  53.6 us (9%)
  matrix products  45.9 us (7%)
  starting transfers between devices  16.8 us (3%)
  between operations  14.5 us (2%)
    all_to_all x1, waiting for transfers between devices, shards(): lax.all_to_all(jnp.stack([qkvg_blocks] * lax.axis_size('row')), 'row', 0, 0)  97.8 us
    reduce_scatter x1, waiting for transfers between devices, shards(): lax.psum_scatter(partial_feed.astype(jnp.bfloat16), 'col', scatter_dimens...  82.6 us
    all_gather x1, waiting for transfers between devices, shards(): normed_mid = lax.all_gather(normed_share, 'col', axis=1, tiled=True)  76.5 us
    unnamed x5, other arithmetic  67 us
    reduce_scatter x1, waiting for transfers between devices, shards(): lax.psum_scatter(partial_mix.astype(jnp.bfloat16), 'col', scatter_dimensi...  60.2 us
    all_gather x1, waiting for transfers between devices, shards(): lax.all_gather(down_blocks, 'row', axis=1, tiled=True)  23.5 us
    psum x1, blocking collectives, shards(): squares = lax.psum(jnp.sum(residual * residual, axis=1), 'col')  21.3 us
    all_to_all x1, blocking collectives, shards(): lax.all_to_all(gateup_master.astype(jnp.bfloat16), 'col', split_axis=2, c...  19.3 us
  transfers between devices with their start and end apart: 10, of which 7 were waited for; matrix products, arithmetic and copies ran while one was open for 27% of the time, Pallas kernels for 0%

profile of v1, /device:TPU:0, one launch (start us, length us, event | category | flops | bytes accessed | tf_op | source)
XLA Modules:
  0.0 622.1 jit_solution(12924808723991642465)
XLA Ops:
  7.2 0.7 all-gather.6.cloned.1.call-update
  7.9 1.2 convert_bitcast_fusion
  9.1 9.8 %copy.81 = bf16[1,16,12288]{1,0,2:T(2,128)(2,1)} copy(bf16[1,16,12288]{2,1,0:T(8,128)(2,1)S(1)} %convert_bitcast_fusion) | data formatting | bytes 786432 | tf_op jit(solution)/shard_map/broadcast_in_dim | solution.py:106
  18.8 0.5 broadcast.313
  19.4 67.0 %reduce.7 = bf16[12288,16]{1,0:T(8,128)(2,1)S(1)} reduce(bf16[12288,1,16]{2,1,0:T(2,128)(2,1)} %bitcast.203, bf16[]{:T(256)} %broadcast.313), dimensions={1}, to_apply=%bitcast.148.reduce_sub_computation | reduce | bytes 786434
  86.4 3.9 reshape.466
  90.3 8.1 %all-to-all-start = ((bf16[8,2,12288]{2,1,0:T(2,128)(2,1)}), bf16[8,2,12288]{2,1,0:T(2,128)(2,1)S(1)}, u32[]{:S(2)}, u32[]{:S(2)}) async-start(bf16[8,2,12288]{2,1,0:T(2,128)(2,1)} %reshape.466), calls=%async_computation | async-start | bytes 786432 | tf_op jit(solution)/shard_map/all_to_all | solution.py:105
  98.4 0.7 copy.118
  99.0 9.2 %all-to-all-done = bf16[8,2,12288]{2,1,0:T(2,128)(2,1)S(1)} async-done(((bf16[8,2,12288]{2,1,0:T(2,128)(2,1)}), bf16[8,2,12288]{2,1,0:T(2,128)(2,1)S(1)}, u32[]{:S(2)}, u32[]{:S(2)}) %all-to-all-start) | async-done | bytes 393248 | tf_op jit(solution)/shard_map/all_to_all | solution.py:105
  108.3 3.4 all-to-all-start.2
  111.6 6.2 %reshape.467 = bf16[12288,1,16]{2,1,0:T(2,128)(2,1)} reshape(bf16[8,2,12288]{2,1,0:T(2,128)(2,1)S(1)} %all-to-all-done) | data formatting | bytes 786432
  117.9 11.4 %copy.82 = bf16[1,16,12288]{2,1,0:T(8,128)(2,1)S(1)} copy(bf16[1,16,12288]{1,0,2:T(2,128)(2,1)} %bitcast.204) | data formatting | bytes 786432 | tf_op jit(solution)/shard_map/all_to_all | solution.py:105
  129.6 3.2 stack.3
  132.9 4.6 all-to-all-start.1
  137.7 1.0 multiply_cosine_fusion
  139.0 3.1 fusion.45
  142.1 97.8 %all-to-all-done.1 = bf16[16,128,1536]{2,1,0:T(8,128)(2,1)} async-done(((bf16[16,128,1536]{2,1,0:T(8,128)(2,1)}), bf16[16,128,1536]{2,1,0:T(8,128)(2,1)}, u32[]{:S(2)}, u32[]{:S(2)}) %all-to-all-start.1) | async-done | bytes 6291488 | tf_op jit(solution)/shard_map/all_to_all | solution.py:128
  239.9 10.5 %fusion.52 = bf16[1024,1536]{1,0:T(8,128)(2,1)S(1)} fusion(bf16[2048,1536]{1,0:T(8,128)(2,1)} %bitcast.3, bf16[1024,2048]{1,0:T(8,128)(2,1)} %all-gather.6.cloned.1.call-done, f32[1024]{0:T(1024)S(1)} %add_rsqrt_fusion.1), kind=kOutput, calls=%fused_computation.65 | convolution fusion | flops 6450315264 | bytes 13635584 | tf_op jit(solution)/shard_map/dot_general | solution.py:125
  250.6 1.4 copy-done.5
  252.0 0.3 subtract_convert_fusion
  252.4 18.8 %while.17 = (s32[]{:T(128)}, f32[2,1,256,512]{3,2,0,1:T(8,128)S(1)}, f32[2,1,256]{2,1,0:T(1,128)S(1)}, f32[2,2,256,1,512]{4,2,0,1,3:T(8,128)}, f32[1]{0:T(128)},...) while((s32[]{:T(128)}, ...), condition=%wide.region_4.5_spmd.clone.clone.clone, body=%wide.region_1.4_spmd.clone.clone.clone.sunk | while | flops 1816989184 | bytes 22576332 | solution.py:86
  252.5 0.6 fusion.101
  253.1 0.3 select_bitcast_fusion.2
  253.5 0.3 fusion.100
  253.8 2.0 convolution_bitcast_fusion.3
  255.7 1.3 divide_bitcast_fusion.2
  257.1 1.6 copy.122
  258.6 1.1 constant_dynamic-update-slice_fusion.2
  259.7 2.0 fusion.98
  261.9 0.6 fusion.101
  262.6 0.3 select_bitcast_fusion.2
  262.9 0.3 fusion.100
  263.2 2.0 convolution_bitcast_fusion.3
  265.2 1.3 divide_bitcast_fusion.2
  266.5 1.6 copy.122
  268.1 1.1 constant_dynamic-update-slice_fusion.2
  269.1 2.0 fusion.98
  271.3 2.0 bitcast_reduce_fusion
  273.3 0.2 copy-done
  273.5 0.4 fusion.66
  274.0 2.1 fusion.67
  276.1 6.0 convolution_convert_fusion.1
  282.1 0.3 all-gather.12.cloned.1.call-start
  282.4 0.7 copy-done.10
  283.2 2.7 copy.89
  285.9 2.2 reshape.464
  288.1 19.3 %all_to_all.79 = bf16[8,2,8192]{2,1,0:T(2,128)(2,1)S(1)} all-to-all(bf16[8,2,8192]{2,1,0:T(2,128)(2,1)S(1)} %reshape.464), channel_id=1, replica_groups=mesh['row'=16,'col'=8] {'col'}, dimensions={0} | all-to-all | bytes 524288 | tf_op jit(solution)/shard_map/all_to_all | solution.py:108
  307.4 1.4 reshape.465
  308.8 3.3 copy.90
  312.1 60.2 %reduce-scatter.3.cloned.1.call-done = bf16[1024,256]{1,0:T(8,128)(2,1)} async-done(((bf16[1024,2048]{1,0:T(8,128)(2,1)}), bf16[1024,256]{1,0:T(8,128)(2,1)}) %reduce-scatter.3.cloned.1.call-update) | async-done | bytes 524304 | tf_op jit(solution)/shard_map/reduce_scatter | solution.py:150
  372.3 1.3 multiply_reduce_fusion
  373.6 21.3 %psum.7 = f32[1024]{0:T(1024)S(1)} all-reduce(f32[1024]{0:T(1024)S(1)} %multiply_reduce_fusion), channel_id=1, replica_groups=mesh['row'=16,'col'=8] {'col'}, use_global_device_ids=true, to_apply=%region_9.10 | all-reduce | flops 1024 | bytes 8192 | tf_op jit(solution)/shard_map/psum | solution.py:153
  395.0 2.1 multiply_convert_fusion
  397.2 13.0 %all_to_all.80 = bf16[8,512,16]{1,2,0:T(8,128)(2,1)} all-to-all(bf16[8,512,16]{1,2,0:T(8,128)(2,1)S(1)} %bitcast.228), channel_id=1, replica_groups=mesh['row'=16,'col'=8] {'col'}, dimensions={0} | all-to-all | bytes 262144 | tf_op jit(solution)/shard_map/all_to_all | solution.py:118
  410.2 0.8 all-gather.12.cloned.1.call-done
  411.0 76.5 %all-gather.10.cloned.1.call-done = bf16[1024,2048]{1,0:T(8,128)(2,1)} async-done(((bf16[1024,256]{1,0:T(8,128)(2,1)}), bf16[1024,2048]{1,0:T(8,128)(2,1)}) %all-gather.10.cloned.1.call-update) | async-done | bytes 4194320 | tf_op jit(solution)/shard_map/all_gather | solution.py:155
  487.5 9.9 %fusion.55 = f32[2,1024,512]{2,1,0:T(8,128)} fusion(bf16[2,2048,512]{2,1,0:T(8,128)(2,1)} %all-gather.12.cloned.1.call-done, bf16[1024,2048]{1,0:T(8,128)(2,1)} %all-gather.10.cloned.1.call-done), kind=kOutput, calls=%fused_computation.70 | convolution fusion | flops 4294967296 | bytes 12582912 | tf_op jit(solution)/shard_map/td,gdf->gtf/dot_general | solution.py:157
  497.4 23.5 %all-gather.14.cloned.1.call-done = bf16[512,2048]{0,1:T(8,128)(2,1)} async-done(((bf16[512,128]{0,1:T(8,128)(2,1)}), bf16[512,2048]{0,1:T(8,128)(2,1)}) %all-gather.14.cloned.1.call-update) | async-done | bytes 2097168 | tf_op jit(solution)/shard_map/all_gather | solution.py:166
  520.9 7.2 %convolution_convert_fusion = bf16[1024,2048]{1,0:T(8,128)(2,1)} fusion(bf16[512,2048]{0,1:T(8,128)(2,1)} %all-gather.14.cloned.1.call-done, f32[2,1024,512]{2,1,0:T(8,128)} %fusion.55), kind=kOutput, calls=%fused_computation.66 | convolution fusion | flops 2152726528 | bytes 10485760 | tf_op jit(solution)/shard_map/dot_general | solution.py:164
  528.2 0.6 copy-done.13
  529.1 0.8 copy.92
  529.8 0.8 copy.93
  530.6 82.6 %reduce-scatter.5.cloned.1.call-done = bf16[1024,256]{1,0:T(8,128)(2,1)} async-done(((bf16[1024,2048]{1,0:T(8,128)(2,1)}), bf16[1024,256]{1,0:T(8,128)(2,1)}) %reduce-scatter.5.cloned.1.call-update) | async-done | bytes 524304 | tf_op jit(solution)/shard_map/reduce_scatter | solution.py:169
  613.1 2.1 select_convert_fusion
  (75 shorter events, 2.0 us)
Async XLA Ops:
  7.2 131.8 %all-gather.6.cloned.1.call-start = ((), (), s32[]{:S(2)}) async-start(), calls=%async_computation.7 | async-start | bytes 4718592 | tf_op jit(solution)/shard_map/all_gather | solution.py:122
  86.3 12.0 %copy-start.11 = (f32[4096,16]{0,1:T(8,128)S(1)}, f32[4096,16]{0,1:T(8,128)}, u32[]{:S(2)}) copy-start(f32[4096,16]{0,1:T(8,128)} %param.12) | copy-start | bytes 786436
  90.3 18.0 %all-to-all-start = ((bf16[8,2,12288]{2,1,0:T(2,128)(2,1)}), bf16[8,2,12288]{2,1,0:T(2,128)(2,1)S(1)}, u32[]{:S(2)}, u32[]{:S(2)}) async-start(bf16[8,2,12288]{2,1,0:T(2,128)(2,1)} %reshape.466), calls=%async_computation | async-start | bytes 786432 | tf_op jit(solution)/shard_map/all_to_all | solution.py:105
  108.3 21.3 %all-to-all-start.2 = ((bf16[8,512,16]{1,2,0:T(8,128)(2,1)}), bf16[8,512,16]{1,2,0:T(8,128)(2,1)S(1)}, u32[]{:S(2)}, u32[]{:S(2)}) async-start(bf16[8,512,16]{1,2,0:T(8,128)(2,1)} %bitcast.161), calls=%async_computation.2 | async-start | bytes 262144 | tf_op jit(solution)/shard_map/all_to_all | solution.py:115
  129.6 3.3 copy-start.6
  129.6 3.2 copy-start.7
  132.9 107.0 %all-to-all-start.1 = ((bf16[16,128,1536]{2,1,0:T(8,128)(2,1)}), bf16[16,128,1536]{2,1,0:T(8,128)(2,1)}, u32[]{:S(2)}, u32[]{:S(2)}) async-start(bf16[16,128,1536]{2,1,0:T(8,128)(2,1)} %stack.3), calls=%async_computation.1 | async-start | bytes 12582912 | tf_op jit(solution)/shard_map/all_to_all | solution.py:128
  137.5 138.6 %all-gather.8.cloned.1.call-start = ((), (), s32[]{:S(2)}) async-start(), calls=%async_computation.8 | async-start | bytes 2228224 | tf_op jit(solution)/shard_map/all_gather | solution.py:147
  138.7 233.6 %reduce-scatter.3.cloned.1.call-start = ((), (), s32[]{:S(2)}) async-start(), calls=%async_computation.9 | async-start | bytes 4718592 | tf_op jit(solution)/shard_map/reduce_scatter | solution.py:150
  250.4 1.6 copy-start.5
  252.4 3.3 copy-start.1
  259.7 2.1 copy-start.2
  261.9 3.3 copy-start.1
  269.1 2.1 copy-start.2
  271.3 2.2 copy-start
  282.1 1.0 copy-start.10
  282.1 128.9 %all-gather.12.cloned.1.call-start = ((), (), s32[]{:S(2)}) async-start(), calls=%async_computation.11 | async-start | bytes 4456448 | tf_op jit(solution)/shard_map/all_gather | solution.py:160
  307.4 65.0 %copy-start.3 = (bf16[1024,256]{1,0:T(8,128)(2,1)S(1)}, bf16[1024,256]{1,0:T(8,128)(2,1)}, u32[]{:S(2)}) copy-start(bf16[1024,256]{1,0:T(8,128)(2,1)} %param.8) | copy-start | bytes 1572868
  312.1 85.1 %copy-start.12 = (f32[4096,16]{0,1:T(8,128)S(1)}, f32[4096,16]{0,1:T(8,128)}, u32[]{:S(2)}) copy-start(f32[4096,16]{0,1:T(8,128)} %param.13) | copy-start | bytes 786436
  312.1 175.4 %all-gather.10.cloned.1.call-start = ((), (), s32[]{:S(2)}) async-start(), calls=%async_computation.10 | async-start | bytes 4718592 | tf_op jit(solution)/shard_map/all_gather | solution.py:155
  397.1 123.9 %all-gather.14.cloned.1.call-start = ((), (), s32[]{:S(2)}) async-start(), calls=%async_computation.12 | async-start | bytes 2228224 | tf_op jit(solution)/shard_map/all_gather | solution.py:166
  410.2 203.0 %reduce-scatter.5.cloned.1.call-start = ((), (), s32[]{:S(2)}) async-start(), calls=%async_computation.13 | async-start | bytes 4718592 | tf_op jit(solution)/shard_map/reduce_scatter | solution.py:169
  528.1 0.7 copy-start.13
  528.1 0.9 copy-start.8
  528.1 1.7 copy-start.9
  528.1 85.0 %copy-start.4 = (bf16[1024,256]{1,0:T(8,128)(2,1)S(1)}, bf16[1024,256]{1,0:T(8,128)(2,1)}, u32[]{:S(2)}) copy-start(bf16[1024,256]{1,0:T(8,128)(2,1)} %reduce-scatter.3.cloned.1.call-done) | copy-start | bytes 1572868
Sparse Core Ops, SparseCore 0:
  10.2 76.3 all-gather.5
  140.6 92.9 all-gather.7
  282.2 90.0 reduce-scatter.2
  374.5 36.4 all-gather.11
  413.9 73.5 all-gather.9
  489.2 31.7 all-gather.13
  528.3 84.7 reduce-scatter.4
